TPU v7x, 1024 devices: a whole 4x8x16 slice. The times are simulated.
1024 devices in a mesh: ctx: 64 (over y_lo, z, core), fsdp: 16 (over y_hi, x).
Axes of the slice: x: 4, y: 8 (y_hi: 4, y_lo: 2; y = y_hi * 2 + y_lo), z: 16, core: 2. Of those that a mesh axis runs over, the one named last changes fastest.
Arguments:
- latents: bfloat16 [16, 8192, 4096], P('fsdp', 'ctx'), may hold values from -6 to 6
- queries: bfloat16 [16, 8192, 2048], P('fsdp', 'ctx')
- values: bfloat16 [16, 8192, 512], P('fsdp', 'ctx'), may hold values from -6 to 6
- d_out: bfloat16 [16, 8192, 2048], P('fsdp', 'ctx'), may hold values from -6 to 6
- w_key: bfloat16 [4096, 512], P('fsdp'), may hold values from -0.09375 to 0.09375
- doc_first: int32 [16, 8192], P('fsdp', 'ctx'), may hold values from 0 to 8191, as said below
Outputs:
- attended: bfloat16 [16, 8192, 2048], P('fsdp', 'ctx')
- grad_query: bfloat16 [16, 8192, 2048], P('fsdp', 'ctx')
- grad_value: bfloat16 [16, 8192, 512], P('fsdp', 'ctx')
- grad_weight: float32 [4096, 512], P('fsdp')
Inputs may be any that keep to these rules, and one draw needn't show every extreme that they name: Non-decreasing along each sequence; doc_first[i] <= i, equal to i exactly at a document's first latent, the same for all latents of a document; the first and the last latent of each sequence begin documents.
All inputs are finite; a program needn't handle non-finite values.
Results may differ from a plain program's by a relative error of at most 0.038.
Values may be sent and summed in bfloat16 or wider, within the bound.
No kernel may reach another device: no remote copies, remote signals or barrier semaphores. Data moves between devices by JAX's collectives and lax.ppermute only.
A program may use at most 64 MiB of HBM per device.

v0:
```python
import jax
import jax.numpy as jnp
from jax import lax
from jax.sharding import PartitionSpec as P

HEADS = 16
KV_HEADS = 4
HEAD_DIM = 128


def from_behind(shard, axis, by):
    count = lax.axis_size(axis)
    pairs = [(i, i + by) for i in range(count) if 0 <= i + by < count]
    return lax.ppermute(shard, axis, pairs)


def attend_block(query_heads, key_heads, value_heads, grad_heads, visible, score_scale):
    scores = (
        jnp.einsum("rkgd,skd->kgrs", query_heads, key_heads, preferred_element_type=jnp.float32)
        * score_scale
    )
    scores = jnp.where(visible, scores, -jnp.inf)
    row_top = jnp.max(scores, axis=-1, keepdims=True)
    weights = jnp.exp(scores - row_top)
    probs = weights / jnp.sum(weights, axis=-1, keepdims=True)
    probs_low = probs.astype(jnp.bfloat16)
    attended = jnp.einsum(
        "kgrs,skd->rkgd", probs_low, value_heads, preferred_element_type=jnp.float32
    ).astype(jnp.bfloat16)
    grad_probs = jnp.einsum(
        "rkgd,skd->kgrs", grad_heads, value_heads, preferred_element_type=jnp.float32
    )
    row_delta = jnp.sum(grad_heads.astype(jnp.float32) * attended.astype(jnp.float32), axis=-1)
    row_delta = jnp.transpose(row_delta, (1, 2, 0))[..., None]
    grad_scores = (probs * (grad_probs - row_delta) * score_scale).astype(jnp.bfloat16)
    grad_query = jnp.einsum(
        "kgrs,skd->rkgd", grad_scores, key_heads, preferred_element_type=jnp.float32
    ).astype(jnp.bfloat16)
    grad_keys = jnp.einsum(
        "kgrs,rkgd->skd", grad_scores, query_heads, preferred_element_type=jnp.float32
    )
    grad_values = jnp.einsum(
        "kgrs,rkgd->skd", probs_low, grad_heads, preferred_element_type=jnp.float32
    )
    return (attended, grad_query, grad_keys, grad_values)


def sum_blocks(block_grad):
    return lax.psum(block_grad, "ctx")


def body(latents, queries, values, d_out, w_key, doc_first):
    rows = latents.shape[1]
    kv_width = values.shape[2]
    groups = HEADS // KV_HEADS
    score_scale = HEAD_DIM ** (-0.5)
    tokens = latents[0]
    columns = tokens
    keys = jnp.dot(
        columns,
        lax.all_gather(w_key, "fsdp", axis=0, tiled=True),
        preferred_element_type=jnp.float32,
    ).astype(jnp.bfloat16)
    own_values = values[0]
    prev_keys, prev_values = from_behind((keys, own_values), "ctx", 1)
    cycle_index = lax.axis_index("ctx")
    query_place = cycle_index * rows + jnp.arange(rows, dtype=jnp.int32)
    key_place = (cycle_index - 1) * rows + jnp.arange(2 * rows, dtype=jnp.int32)
    visible = (key_place[None, :] <= query_place[:, None]) & (
        key_place[None, :] >= doc_first[0][:, None]
    )
    query_heads = queries[0].reshape(rows, KV_HEADS, groups, HEAD_DIM)
    grad_heads = d_out[0].reshape(rows, KV_HEADS, groups, HEAD_DIM)

    def split_heads(block):
        return block.reshape(block.shape[0], KV_HEADS, HEAD_DIM)

    key_heads = split_heads(jnp.concatenate([prev_keys, keys], axis=0))
    value_heads = split_heads(jnp.concatenate([prev_values, own_values], axis=0))
    attended, grad_query, grad_keys, grad_values = attend_block(
        query_heads, key_heads, value_heads, grad_heads, visible, score_scale
    )
    own_key_grad = grad_keys[rows:]
    own_value_grad = grad_values[rows:]
    back_key_grad = grad_keys[:rows].astype(jnp.bfloat16)
    back_value_grad = grad_values[:rows].astype(jnp.bfloat16)
    next_key_grad, next_value_grad = from_behind((back_key_grad, back_value_grad), "ctx", -1)
    grad_key = (
        (own_key_grad + next_key_grad.astype(jnp.float32))
        .reshape(rows, kv_width)
        .astype(jnp.bfloat16)
    )
    grad_value = (
        (own_value_grad + next_value_grad.astype(jnp.float32))
        .reshape(rows, kv_width)
        .astype(jnp.bfloat16)
    )
    columns = tokens
    block_grad = lax.psum_scatter(
        lax.dot_general(
            columns, grad_key, (((0,), (0,)), ((), ())), preferred_element_type=jnp.float32
        ).astype(jnp.bfloat16),
        "fsdp",
        scatter_dimension=0,
        tiled=True,
    ).astype(jnp.float32)
    grad_weight = sum_blocks(block_grad)
    return (
        attended.reshape(1, rows, HEADS * HEAD_DIM),
        grad_query.reshape(1, rows, HEADS * HEAD_DIM),
        grad_value[None],
        grad_weight,
    )


def solution(mesh):
    placed = (
        P("fsdp", "ctx", None),
        P("fsdp", "ctx", None),
        P("fsdp", "ctx", None),
        P("fsdp", "ctx", None),
        P("fsdp", None),
        P("fsdp", "ctx"),
    )
    return jax.shard_map(
        body,
        mesh=mesh,
        in_specs=placed,
        out_specs=(
            P("fsdp", "ctx", None),
            P("fsdp", "ctx", None),
            P("fsdp", "ctx", None),
            P("fsdp", None),
        ),
        check_vma=False,
    )
```

profile of v0, /device:TPU:6, one launch (start us, length us, event | category | flops | bytes accessed | tf_op | source)
XLA Modules:
  0.0 472.6 jit_solution(8682981682326218372)
XLA Ops:
  7.2 0.0 copy-start
  7.2 0.0 all-gather.2.cloned.1.call-start
  7.2 0.7 all-gather.2.cloned.1.call-update
  7.9 0.0 reduce-scatter.2.cloned.1.call-start
  8.0 1.7 collective-permute-start
  9.7 1.0 copy.11
  10.8 1.3 copy.44
  12.1 1.3 copy.15
  13.4 0.0 copy-start.5
  13.4 95.3 %all-gather.2.cloned.1.call-done = bf16[4096,512]{1,0:T(8,128)(2,1)} async-done(((bf16[256,512]{1,0:T(8,128)(2,1)}), bf16[4096,512]{1,0:T(8,128)(2,1)}) %all-gather.2.cloned.1.call-update) | async-done | bytes 4194320 | tf_op jit(solution)/shard_map/all_gather | solution.py:61
  108.8 0.0 copy-done
  108.8 2.9 convolution_convert_fusion.3
  111.7 1.7 collective-permute-start.1
  113.4 0.0 copy-done.5
  113.4 0.1 compare_and_fusion
  113.5 0.0 collective-permute-done
  113.6 0.1 copy.10
  113.7 0.0 copy-start.4
  113.7 0.7 collective-permute-done.1
  114.4 0.1 reshape.47
  114.5 0.2 copy.32
  114.7 2.1 fusion.22
  116.8 2.9 multiply_reduce_fusion
  119.7 0.0 copy-done.4
  119.7 0.0 copy-done.6
  119.7 1.5 fusion.4
  121.2 0.5 convolution_bitcast_fusion
  121.7 1.3 collective-permute-start.3
  123.0 4.3 collective-permute-done.3
  127.3 3.2 fusion.1
  130.5 0.0 reduce-scatter.2.cloned.1.call-update
  130.5 2.1 convolution_bitcast_fusion.1
  132.6 0.0 copy-start.2
  132.6 0.0 copy-start.1
  132.7 0.8 copy-done.2
  133.4 1.3 collective-permute-start.2
  134.7 0.3 convolution_convert_fusion.1
  135.0 0.0 copy-start.3
  135.0 1.0 copy.24
  136.1 0.0 copy-done.1
  136.1 1.0 copy.23
  137.1 3.5 collective-permute-done.2
  140.5 0.0 copy-done.3
  140.5 0.9 fusion.13
  141.5 0.8 copy.25
  142.3 106.5 %reduce-scatter.2.cloned.1.call-done = bf16[256,512]{0,1:T(8,128)(2,1)} async-done(((bf16[4096,512]{0,1:T(8,128)(2,1)}), bf16[256,512]{0,1:T(8,128)(2,1)}) %reduce-scatter.2.cloned.1.call-update) | async-done | bytes 262160 | tf_op jit(solution)/shard_map/reduce_scatter | solution.py:99
  248.7 216.1 %all-reduce.1 = f32[256,512]{0,1:T(8,128)S(1)} all-reduce(bf16[256,512]{0,1:T(8,128)(2,1)} %reduce-scatter.2.cloned.1.call-done), channel_id=1, replica_groups=mesh['ctx'=64,'fsdp'=16] {'ctx'}, use_global_device_ids=true, to_apply=%region_4.5 | all-reduce | flops 131072 | bytes 786432 | tf_op jit(solution)/shard_map/psum | solution.py:49
  464.8 1.0 copy.26
  (7 shorter events, 0.1 us)
Async XLA Ops:
  7.2 101.6 %copy-start = (bf16[1,128,4096]{2,1,0:T(8,128)(2,1)S(1)}, bf16[1,128,4096]{2,1,0:T(8,128)(2,1)}, u32[]{:S(2)}) copy-start(bf16[1,128,4096]{2,1,0:T(8,128)(2,1)} %param.6) | copy-start | bytes 3145732
  7.2 101.6 %all-gather.2.cloned.1.call-start = ((), (), s32[]{:S(2)}) async-start(), calls=%async_computation.1 | async-start | bytes 4456448 | tf_op jit(solution)/shard_map/all_gather | solution.py:61
  7.9 240.8 %reduce-scatter.2.cloned.1.call-start = ((), (), s32[]{:S(2)}) async-start(), calls=%async_computation.2 | async-start | bytes 4456448 | tf_op jit(solution)/shard_map/reduce_scatter | solution.py:99
  8.0 105.6 %collective-permute-start = (bf16[128,512]{1,0:T(8,128)(2,1)}, bf16[128,512]{1,0:T(8,128)(2,1)S(1)}, u32[]{:S(2)}, u32[]{:S(2)}) collective-permute-start(bf16[128,512]{1,0:T(8,128)(2,1)} %bitcast.81), channel_id=1, source_target_pairs={{0,16},{16,32},{32,48},{48,64},{64,80},{80,96},{96,112},{112,128},... | collective-permute-start | bytes 393224 | tf_op jit(solution)/shard_map/ppermute | solution.py:14
  13.4 100.0 %copy-start.5 = (s32[1,128]{1,0:T(1,128)S(1)}, s32[1,128]{1,0:T(1,128)}, u32[]{:S(2)}) copy-start(s32[1,128]{1,0:T(1,128)} %param.11) | copy-start | bytes 1540
  111.7 2.7 collective-permute-start.1
  113.7 6.0 %copy-start.4 = (bf16[128,512]{0,1:T(8,128)(2,1)}, bf16[128,512]{0,1:T(8,128)(2,1)S(1)}, u32[]{:S(2)}) copy-start(bf16[128,512]{0,1:T(8,128)(2,1)S(1)} %copy.10) | copy-start | bytes 393220
  116.8 2.9 copy-start.6
  121.7 5.6 %collective-permute-start.3 = (bf16[128,4,128]{0,2,1:T(8,128)(2,1)S(1)}, bf16[128,4,128]{0,2,1:T(8,128)(2,1)S(1)}, u32[]{:S(2)}, u32[]{:S(2)}) collective-permute-start(bf16[128,4,128]{0,2,1:T(8,128)(2,1)S(1)} %slice.30), channel_id=1, source_target_pairs={{16,0},{32,16},{48,32},{64,48},{80,64},{96,80},{112,96},{128,112},... | collective-permute-start | bytes 393224 | tf_op jit(solution)/shard_map/ppermute | solution.py:14
  132.6 0.8 copy-start.2
  132.6 3.4 copy-start.1
  133.4 7.1 %collective-permute-start.2 = (bf16[128,4,128]{0,2,1:T(8,128)(2,1)S(1)}, bf16[128,4,128]{0,2,1:T(8,128)(2,1)}, u32[]{:S(2)}, u32[]{:S(2)}) collective-permute-start(bf16[128,4,128]{0,2,1:T(8,128)(2,1)S(1)} %slice.31), channel_id=1, source_target_pairs={{16,0},{32,16},{48,32},{64,48},{80,64},{96,80},{112,96},{128,112},... | collective-permute-start | bytes 393224 | tf_op jit(solution)/shard_map/ppermute | solution.py:14
  135.0 5.5 %copy-start.3 = (f32[256,4,128]{0,2,1:T(8,128)S(1)}, f32[256,4,128]{0,2,1:T(8,128)}, u32[]{:S(2)}) copy-start(f32[256,4,128]{0,2,1:T(8,128)} %copy-done.2) | copy-start | bytes 1572868
Sparse Core Ops, SparseCore 0:
  12.2 96.5 all-gather.1
  130.7 118.0 reduce-scatter.1
where the time goes:
time: 473 us
  blocking collectives  216 us (46%)
  waiting for transfers between devices  211 us (45%)
  matrix products  15.4 us (3%)
  between operations  14.3 us (3%)
  local copies, waits for them, and re-layouts  8.64 us (2%)
  starting transfers between devices  6.14 us (1%)
    psum x1, blocking collectives, sum_blocks(): return lax.psum(block_grad, 'ctx')  216 us
    reduce_scatter x1, waiting for transfers between devices, body(): lax.psum_scatter(lax.dot_general(columns, grad_key, (((0,), (0,)), ((), (...  106 us
    all_gather x1, waiting for transfers between devices, body(): lax.all_gather(w_key, 'fsdp', axis=0, tiled=True)  95.3 us
  transfers between devices with their start and end apart: 6, of which 5 were waited for; matrix products, arithmetic and copies ran while one was open for 3% of the time, Pallas kernels for 0%

commit v1 on v0

v1 whole, which is shorter than its diff:
```python
import jax
import jax.numpy as jnp
from jax import lax
from jax.experimental import pallas as pl
from jax.experimental.pallas import tpu as pltpu
from jax.sharding import Mesh, PartitionSpec as P

HEADS = 16
KV_HEADS = 4
GROUPS = HEADS // KV_HEADS
HEAD_DIM = 128
ROWS = 128
AXES = ("ylo", "z", "core", "yhi", "x")
CTX = ("ylo", "z", "core")


def exchange(parts, axis):
    return lax.all_to_all(parts, axis, 0, 0, tiled=True)


def gather(part, axis):
    return exchange(jnp.broadcast_to(part[None], (lax.axis_size(axis),) + part.shape), axis)


def shift(shard, axis, by):
    count = lax.axis_size(axis)
    return lax.ppermute(shard, axis, [(i, i + by) for i in range(count) if 0 <= i + by < count])


def swap(shard):
    return lax.ppermute(shard, "core", [(0, 1), (1, 0)])


def dot(a, b, contract):
    return lax.dot_general(a, b, ((contract[:1], contract[1:]), ((), ())), preferred_element_type=jnp.float32)


def attend_kernel(place_ref, first_ref, q_ref, g_ref, kp_ref, ko_ref, vp_ref, vo_ref, att_ref, gq_ref, gk_ref, gv_ref):
    scale = HEAD_DIM ** -0.5
    start = place_ref[0]
    row = start + lax.broadcasted_iota(jnp.int32, (ROWS, 2 * ROWS), 0)
    col = start - ROWS + lax.broadcasted_iota(jnp.int32, (ROWS, 2 * ROWS), 1)
    seen = (col <= row) & (col >= first_ref[...])
    bias = jnp.where(seen, 0.0, -jnp.inf)
    bias = jnp.concatenate([bias] * GROUPS, axis=0)
    for k in range(KV_HEADS):
        kv = slice(k * HEAD_DIM, (k + 1) * HEAD_DIM)
        heads = [slice((k * GROUPS + g) * HEAD_DIM, (k * GROUPS + g + 1) * HEAD_DIM) for g in range(GROUPS)]
        q = jnp.concatenate([q_ref[:, h] for h in heads], axis=0)
        g = jnp.concatenate([g_ref[:, h] for h in heads], axis=0)
        keys = jnp.concatenate([kp_ref[:, kv], ko_ref[:, kv]], axis=0)
        values = jnp.concatenate([vp_ref[:, kv], vo_ref[:, kv]], axis=0)
        s = dot(q, keys, (1, 1)) * scale + bias
        w = jnp.exp(s - jnp.max(s, axis=1, keepdims=True))
        p = w / jnp.sum(w, axis=1, keepdims=True)
        low = p.astype(jnp.bfloat16)
        att = dot(low, values, (1, 0)).astype(jnp.bfloat16)
        delta = jnp.sum(g.astype(jnp.float32) * att.astype(jnp.float32), axis=1, keepdims=True)
        ds = (p * (dot(g, values, (1, 1)) - delta) * scale).astype(jnp.bfloat16)
        gq = dot(ds, keys, (1, 0)).astype(jnp.bfloat16)
        for i, h in enumerate(heads):
            rows = slice(i * ROWS, (i + 1) * ROWS)
            att_ref[:, h] = att[rows]
            gq_ref[:, h] = gq[rows]
        gk_ref[:, kv] = dot(ds, q, (0, 0))
        gv_ref[:, kv] = dot(low, g, (0, 0))


def attend(place, first, q, g, kp, ko, vp, vo):
    width = KV_HEADS * HEAD_DIM
    vmem = pl.BlockSpec(memory_space=pltpu.VMEM)
    return pl.pallas_call(
        attend_kernel,
        out_shape=(
            jax.ShapeDtypeStruct(q.shape, jnp.bfloat16),
            jax.ShapeDtypeStruct(q.shape, jnp.bfloat16),
            jax.ShapeDtypeStruct((2 * ROWS, width), jnp.float32),
            jax.ShapeDtypeStruct((2 * ROWS, width), jnp.float32),
        ),
        in_specs=[pl.BlockSpec(memory_space=pltpu.SMEM)] + [vmem] * 7,
        out_specs=[vmem] * 4,
        compiler_params=pltpu.CompilerParams(vmem_limit_bytes=32 << 20),
        cost_estimate=pl.CostEstimate(flops=700_000_000, bytes_accessed=4_000_000, transcendentals=600_000),
    )(place, first, q, g, kp, ko, vp, vo)


def body(latents, queries, values, d_out, w_key, doc_first):
    lat = latents[0]
    val = values[0]
    core = lax.axis_index("core")
    width = KV_HEADS * HEAD_DIM
    half = width // 2

    w_half = lax.dynamic_slice_in_dim(w_key, core * half, half, 1)
    w_y = gather(w_half, "yhi").reshape(4, 256, half)
    w_x = gather(w_y, "x").reshape(4, 4, 256, half)
    w_o = swap(w_x)

    lat_prev = shift(lat, CTX, 1)
    val_prev = shift(val, CTX, 1)
    lat_cols = lat.reshape(ROWS, 4, 4, 256).transpose(2, 0, 1, 3).reshape(4, ROWS, 1024)
    lat_x = exchange(lat_cols, "x").reshape(4 * ROWS, 1024)
    lat_o = swap(lat_x)

    both = jnp.concatenate([lat_prev, lat], axis=0).reshape(2 * ROWS, 4, 4, 256)

    def project(w):
        return jnp.einsum("tyxk,xykn->tn", both, w, preferred_element_type=jnp.float32).astype(jnp.bfloat16)

    k_mine, k_other = project(w_x), project(w_o)
    first_half = jnp.where(core == 0, k_mine, k_other)
    second_half = jnp.where(core == 0, k_other, k_mine)
    keys = jnp.concatenate([first_half, second_half], axis=1)

    place = (lax.axis_index(CTX) * ROWS).astype(jnp.int32).reshape(1)
    att, gq, gk, gv = attend(
        place, doc_first.reshape(ROWS, 1), queries[0], d_out[0], keys[:ROWS], keys[ROWS:], val_prev, val
    )
    back = jnp.concatenate([gk[:ROWS], gv[:ROWS]], axis=1).astype(jnp.bfloat16)
    ahead = shift(back, CTX, -1).astype(jnp.float32)
    grad_key = (gk[ROWS:] + ahead[:, :width]).astype(jnp.bfloat16)
    grad_value = (gv[ROWS:] + ahead[:, width:]).astype(jnp.bfloat16)

    halves = grad_key.reshape(ROWS, 2, half).transpose(1, 0, 2)
    sent = jnp.broadcast_to(halves[:, None], (2, 4, ROWS, half)).reshape(8, ROWS, half)
    got = exchange(sent, ("core", "x")).reshape(2, 4 * ROWS, half)
    g_mine = jnp.where(core == 0, got[0], got[1])
    g_other = jnp.where(core == 0, got[1], got[0])
    part = (dot(lat_x, g_mine, (0, 0)) + dot(lat_o, g_other, (0, 0))).astype(jnp.bfloat16)

    part = exchange(part.reshape(8, 128, half), ("yhi", "ylo")).reshape(8, 128, half)
    part = jnp.sum(part.astype(jnp.float32), axis=0).astype(jnp.bfloat16)
    part = exchange(part.reshape(16, 8, half), "z").reshape(16, 8, half)
    part = jnp.sum(part.astype(jnp.float32), axis=0).astype(jnp.bfloat16)
    mine = gather(part, ("ylo", "z")).reshape(256, half)
    other = swap(mine)
    left = jnp.where(core == 0, mine, other)
    right = jnp.where(core == 0, other, mine)
    grad_weight = jnp.concatenate([left, right], axis=1).astype(jnp.float32)
    return att[None], gq[None], grad_value[None], grad_weight


def solution(mesh):
    fine = Mesh(mesh.devices.reshape(2, 16, 2, 4, 4), AXES)
    row, col = ("yhi", "x"), CTX
    block = P(row, col, None)
    return jax.shard_map(
        body,
        mesh=fine,
        in_specs=(block, block, block, block, P(row, None), P(row, col)),
        out_specs=(block, block, block, P(row, None)),
        check_vma=False,
    )
```

time: 473 us -> 187 us (0.40)
  waiting for transfers between devices: 211 us -> 1.33 us
  blocking collectives: 216 us -> 139 us
  starting transfers between devices: 6.14 us -> 21 us
  between operations: 14.3 us -> 0.97 us
  matrix products: 15.4 us -> 7.3 us
    psum x1 -> x0, blocking collectives: 216 us -> none  [sum_blocks(): return lax.psum(block_grad, 'ctx')]
    all_to_all x0 -> x6, blocking collectives: none -> 139 us  [exchange(): return lax.all_to_all(parts, axis, 0, 0, tiled=True)]
    reduce_scatter x1 -> x0, waiting for transfers between devices: 106 us -> none  [body(): lax.psum_scatter(lax.dot_general(columns, grad_key, (((0,), (0,)), ((), (...]
    all_gather x1 -> x0, waiting for transfers between devices: 95.3 us -> none  [body(): lax.all_gather(w_key, 'fsdp', axis=0, tiled=True)]
    ppermute x4 -> x6, starting transfers between devices: 6.06 us -> 15.3 us  [the longest x3 7.69 us: swap(): return lax.ppermute(shard, 'core', [(0, 1), (1, 0)])]
    ppermute x4 -> x6, waiting for transfers between devices: 8.51 us -> 1.33 us  [the longest x3 1.32 us: swap(): return lax.ppermute(shard, 'core', [(0, 1), (1, 0)])]
    dot_general x7 -> x4, matrix products: 13.3 us -> 7.3 us  [the longest x2 5.15 us: project(): jnp.einsum('tyxk,xykn->tn', both, w, preferred_element_type=jnp.float32)]
    all_to_all x0 -> x1, starting transfers between devices: none -> 5.69 us  [exchange(): return lax.all_to_all(parts, axis, 0, 0, tiled=True)]
  transfers between devices with their start and end apart: 6 -> 7, of which waited for: 5 -> 1; matrix products, arithmetic and copies ran while one was open for 3% -> 7% of each run, Pallas kernels for 0% -> 2%
where the time goes in v1:
time: 187 us; the launch traced here: 184 us
  blocking collectives  139 us (74%)
  starting transfers between devices  21 us (11%)
  local copies, waits for them, and re-layouts  7.56 us (4%)
  matrix products  7.3 us (4%)
  Pallas kernels  4.2 us (2%)
    all_to_all x6, blocking collectives, exchange(): return lax.all_to_all(parts, axis, 0, 0, tiled=True)  139 us
    ppermute x3, starting transfers between devices, swap(): return lax.ppermute(shard, 'core', [(0, 1), (1, 0)])  7.69 us
    ppermute x3, starting transfers between devices, shift(): lax.ppermute(shard, axis, [(i, i + by) for i in range(count) if 0 <= i +...  7.62 us
    all_to_all x1, starting transfers between devices, exchange(): return lax.all_to_all(parts, axis, 0, 0, tiled=True)  5.69 us
    dot_general x2, matrix products, project(): jnp.einsum('tyxk,xykn->tn', both, w, preferred_element_type=jnp.float32)  5.15 us
    pallas_call x1, Pallas kernels, attend(): pl.pallas_call(attend_kernel, out_shape=(jax.ShapeDtypeStruct(q.shape, jn...  4.2 us
  transfers between devices with their start and end apart: 7, of which 1 were waited for; matrix products, arithmetic and copies ran while one was open for 7% of the time, Pallas kernels for 2%

profile of v1, /device:TPU:6, one launch (start us, length us, event | category | flops | bytes accessed | tf_op | source)
XLA Modules:
  0.0 183.6 jit_solution(5722960314148387678)
XLA Ops:
  0.6 0.0 copy-start
  0.7 0.9 copy-done
  1.6 0.1 copy.45
  1.7 23.2 %all_to_all.35 = bf16[4,256,256]{1,2,0:T(8,128)(2,1)S(1)} all-to-all(bf16[4,256,256]{1,2,0:T(8,128)(2,1)S(1)} %broadcast_in_dim.14), channel_id=1, replica_groups=mesh['ylo'=2,'z'=16,'core'=2,'yhi'=4,'x'=4] {'yhi'}, dimensions={0} | all-to-all | bytes 1048576 | tf_op jit(solution)/shard_map/all_to_all | solution.py:18
  25.0 0.2 broadcast_in_dim.15
  25.2 0.0 copy-start.4
  25.2 27.6 %all_to_all.36 = bf16[4,4,256,256]{2,3,1,0:T(8,128)(2,1)} all-to-all(bf16[4,4,256,256]{2,3,1,0:T(8,128)(2,1)S(1)} %broadcast_in_dim.15), channel_id=1, replica_groups=mesh['ylo'=2,'z'=16,'core'=2,'yhi'=4,'x'=4] {'x'}, dimensions={0} | all-to-all | bytes 4194304 | tf_op jit(solution)/shard_map/all_to_all | solution.py:18
  52.8 2.0 %collective-permute-start.1 = (bf16[4,4,256,256]{2,3,1,0:T(8,128)(2,1)}, bf16[4,4,256,256]{2,3,1,0:T(8,128)(2,1)}, u32[]{:S(2)}, u32[]{:S(2)}) collective-permute-start(bf16[4,4,256,256]{2,3,1,0:T(8,128)(2,1)} %all_to_all.36), channel_id=1, source_target_pairs={{0,16},{16,0},{1,17},{17,1},{2,18},{18,2},{3,19},{19,3},{4,20},{20... | collective-permute-start | bytes 6291464 | tf_op jit(solution)/shard_map/ppermute | solution.py:31
  54.9 0.0 copy-done.4
  54.9 0.7 copy.41
  55.5 3.4 %collective-permute-start = (bf16[128,4096]{0,1:T(8,128)(2,1)S(1)}, bf16[128,4096]{0,1:T(8,128)(2,1)}, u32[]{:S(2)}, u32[]{:S(2)}) collective-permute-start(bf16[128,4096]{0,1:T(8,128)(2,1)S(1)} %bitcast.48), channel_id=1, source_target_pairs={{0,16},{16,32},{32,48},{48,64},{64,80},{80,96},{96,112},{112,128},... | collective-permute-start | bytes 3145736 | tf_op jit(solution)/shard_map/ppermute | solution.py:27
  58.9 0.0 copy-done.3
  58.9 2.9 %collective-permute-start.2 = (bf16[128,512]{1,0:T(8,128)(2,1)S(1)}, bf16[128,512]{1,0:T(8,128)(2,1)S(1)}, u32[]{:S(2)}, u32[]{:S(2)}) collective-permute-start(bf16[128,512]{1,0:T(8,128)(2,1)S(1)} %bitcast.46), channel_id=1, source_target_pairs={{0,16},{16,32},{32,48},{48,64},{64,80},{80,96},{96,112},{112,128},... | collective-permute-start | bytes 393224 | tf_op jit(solution)/shard_map/ppermute | solution.py:27
  61.9 0.1 copy.50
  62.0 1.3 copy.51
  63.3 5.7 %all-to-all-start.3 = ((bf16[4,128,1024]{2,1,0:T(8,128)(2,1)}), bf16[4,128,1024]{2,1,0:T(8,128)(2,1)S(1)}, u32[]{:S(2)}, u32[]{:S(2)}) async-start(bf16[4,128,1024]{2,1,0:T(8,128)(2,1)} %copy.51), calls=%async_computation.3 | async-start | bytes 2097152 | tf_op jit(solution)/shard_map/all_to_all | solution.py:18
  69.0 1.3 copy.44
  70.3 0.0 copy-done.7
  70.3 0.1 copy.48.first_ref
  70.4 0.0 collective-permute-done
  70.5 0.0 copy-start.5
  70.5 2.4 %copy.43 = bf16[128,4,4,256]{3,0,1,2:T(8,128)(2,1)} copy(bf16[128,4,4,256]{0,3,2,1:T(8,128)(2,1)} %bitcast.5) | data formatting | bytes 2097152 | tf_op jit(solution)/shard_map/concatenate | solution.py:105
  72.8 0.0 copy-done.5
  72.8 2.7 %fusion.7 = bf16[256,256]{1,0:T(8,128)(2,1)S(1)} fusion(bf16[4,4,256,256]{2,3,1,0:T(8,128)(2,1)} %all_to_all.36, bf16[128,4,4,256]{3,0,1,2:T(8,128)(2,1)S(1)} %copy-done.5, bf16[128,4,4,256]{3,0,1,2:T(8,128)(2,1)} %copy.43), kind=kOutput, calls=%fused_computation.10 | convolution fusion | flops 541130752 | bytes 4325376 | tf_op jit(solution)/shard_map/tyxk,xykn->tn/dot_general | solution.py:108
  75.6 0.0 copy-start.1
  75.6 0.0 copy-start.2
  75.6 0.0 collective-permute-done.1
  75.6 2.4 %broadcast_select_fusion.3 = (bf16[256,256]{1,0:T(8,128)(2,1)S(1)}, bf16[256,256]{1,0:T(8,128)(2,1)S(1)}) fusion(bf16[256,256]{1,0:T(8,128)(2,1)S(1)} %fusion.7, pred[]{:T(512)S(6)} %eq.2, bf16[4,4,256,256]{2,3,1,0:T(8,128)(2,1)} %collective-permute-done.1, bf16[128,4,4,256]{3,0,1,2:T(8,128)(2,1)S(1)} %copy-done.5, bf16[128,4,4,256]{3,0,1,2:T(8,128)(2,1)S(1)} %copy-done.6), kind=kOutput, calls=%fused_computation.32 | convolution fusion | flops 541261824 | bytes 4587521 | tf_op jit(solution)/shard_map/tyxk,xykn->tn/dot_general | solution.py:108
  78.1 0.0 collective-permute-done.2.vp_ref
  78.1 4.2 %shard_map.93 = (bf16[128,2048]{1,0:T(8,128)(2,1)}, bf16[128,2048]{1,0:T(8,128)(2,1)}, f32[256,512]{1,0:T(8,128)S(1)}, f32[256,512]{1,0:T(8,128)S(1)}) custom-call(s32[1]{0:T(128)} %bitcast.place_ref, s32[128,1]{1,0:T(8,128)S(1)} %copy.48.first_ref, bf16[128,2048]{1,0:T(8,128)(2,1)S(1)} %bitcast.44, bf16[128,2048]{1,0:T(8,128)(2,1)S(1)} %bitcast.45, ...), custom_call_target="tpu_custom_call" | custom-call | flops 700000000 | bytes 4000000 | tf_op jit(solution)/shard_map/pallas_call | solution.py:72
  82.4 1.3 collective-permute-start.3
  83.7 0.0 all-to-all-done.3
  83.7 3.7 %collective-permute-start.4 = (bf16[512,1024]{1,0:T(8,128)(2,1)S(1)}, bf16[512,1024]{1,0:T(8,128)(2,1)}, u32[]{:S(2)}, u32[]{:S(2)}) collective-permute-start(bf16[512,1024]{1,0:T(8,128)(2,1)S(1)} %bitcast.51), channel_id=1, source_target_pairs={{0,16},{16,0},{1,17},{17,1},{2,18},{18,2},{3,19},{19,3},{4,20},{20... | collective-permute-start | bytes 3145736 | tf_op jit(solution)/shard_map/ppermute | solution.py:31
  87.4 0.0 collective-permute-done.3
  87.5 0.7 fusion.8
  88.3 16.9 %all_to_all.37 = bf16[8,128,256]{2,1,0:T(8,128)(2,1)S(1)} all-to-all(bf16[8,128,256]{2,1,0:T(8,128)(2,1)S(1)} %bitcast.53), channel_id=1, replica_groups=mesh['ylo'=2,'z'=16,'core'=2,'yhi'=4,'x'=4] {'core','x'}, dimensions={0} | all-to-all | bytes 1048576 | tf_op jit(solution)/shard_map/all_to_all | solution.py:18
  105.2 0.5 convolution_bitcast_fusion
  105.7 0.0 collective-permute-done.4
  105.7 1.7 fusion.3
  107.4 0.1 copy.64
  107.5 34.7 %all_to_all.38 = bf16[8,128,256]{1,2,0:T(8,128)(2,1)S(1)} all-to-all(bf16[8,128,256]{1,2,0:T(8,128)(2,1)S(1)} %bitcast.54), channel_id=1, replica_groups=mesh['ylo'=2,'z'=16,'core'=2,'yhi'=4,'x'=4] {'yhi','ylo'}, dimensions={0} | all-to-all | bytes 1048576 | tf_op jit(solution)/shard_map/all_to_all | solution.py:18
  142.2 0.1 reduce_sum.24
  142.3 0.1 copy.55
  142.4 18.4 %all_to_all.39 = bf16[16,8,256]{2,1,0:T(8,128)(2,1)S(1)} all-to-all(bf16[16,8,256]{2,1,0:T(8,128)(2,1)S(1)} %bitcast.58), channel_id=1, replica_groups=mesh['ylo'=2,'z'=16,'core'=2,'yhi'=4,'x'=4] {'z'}, dimensions={0} | all-to-all | bytes 131072 | tf_op jit(solution)/shard_map/all_to_all | solution.py:18
  160.8 18.6 %all_to_all.40 = bf16[32,8,256]{2,1,0:T(8,128)(2,1)S(1)} all-to-all(bf16[32,8,256]{2,1,0:T(8,128)(2,1)S(1)} %broadcast_in_dim.39), channel_id=1, replica_groups=mesh['ylo'=2,'z'=16,'core'=2,'yhi'=4,'x'=4] {'ylo','z'}, dimensions={0} | all-to-all | bytes 262144 | tf_op jit(solution)/shard_map/all_to_all | solution.py:18
  179.5 1.9 %collective-permute-start.5 = (bf16[256,256]{1,0:T(8,128)(2,1)S(1)}, bf16[256,256]{1,0:T(8,128)(2,1)S(1)}, u32[]{:S(2)}, u32[]{:S(2)}) collective-permute-start(bf16[256,256]{1,0:T(8,128)(2,1)S(1)} %bitcast.56), channel_id=1, source_target_pairs={{0,16},{16,0},{1,17},{17,1},{2,18},{18,2},{3,19},{19,3},{4,20},{20... | collective-permute-start | bytes 393224 | tf_op jit(solution)/shard_map/ppermute | solution.py:31
  181.4 1.3 collective-permute-done.5
  182.7 0.9 maximum_convert_fusion
  (20 shorter events, 0.3 us)
Async XLA Ops:
  0.6 1.0 copy-start
  25.2 29.7 %copy-start.4 = (bf16[1,128,4096]{2,1,0:T(8,128)(2,1)S(1)}, bf16[1,128,4096]{2,1,0:T(8,128)(2,1)}, u32[]{:S(2)}) copy-start(bf16[1,128,4096]{2,1,0:T(8,128)(2,1)} %param.6) | copy-start | bytes 3145732
  52.8 6.1 %copy-start.3 = (bf16[1,128,512]{2,1,0:T(8,128)(2,1)S(1)}, bf16[1,128,512]{2,1,0:T(8,128)(2,1)}, u32[]{:S(2)}) copy-start(bf16[1,128,512]{2,1,0:T(8,128)(2,1)} %param.8) | copy-start | bytes 393220
  52.8 22.8 %collective-permute-start.1 = (bf16[4,4,256,256]{2,3,1,0:T(8,128)(2,1)}, bf16[4,4,256,256]{2,3,1,0:T(8,128)(2,1)}, u32[]{:S(2)}, u32[]{:S(2)}) collective-permute-start(bf16[4,4,256,256]{2,3,1,0:T(8,128)(2,1)} %all_to_all.36), channel_id=1, source_target_pairs={{0,16},{16,0},{1,17},{17,1},{2,18},{18,2},{3,19},{19,3},{4,20},{20... | collective-permute-start | bytes 6291464 | tf_op jit(solution)/shard_map/ppermute | solution.py:31
  55.5 14.9 %collective-permute-start = (bf16[128,4096]{0,1:T(8,128)(2,1)S(1)}, bf16[128,4096]{0,1:T(8,128)(2,1)}, u32[]{:S(2)}, u32[]{:S(2)}) collective-permute-start(bf16[128,4096]{0,1:T(8,128)(2,1)S(1)} %bitcast.48), channel_id=1, source_target_pairs={{0,16},{16,32},{32,48},{48,64},{64,80},{80,96},{96,112},{112,128},... | collective-permute-start | bytes 3145736 | tf_op jit(solution)/shard_map/ppermute | solution.py:27
  58.9 19.1 %collective-permute-start.2 = (bf16[128,512]{1,0:T(8,128)(2,1)S(1)}, bf16[128,512]{1,0:T(8,128)(2,1)S(1)}, u32[]{:S(2)}, u32[]{:S(2)}) collective-permute-start(bf16[128,512]{1,0:T(8,128)(2,1)S(1)} %bitcast.46), channel_id=1, source_target_pairs={{0,16},{16,32},{32,48},{48,64},{64,80},{80,96},{96,112},{112,128},... | collective-permute-start | bytes 393224 | tf_op jit(solution)/shard_map/ppermute | solution.py:27
  63.3 7.0 %copy-start.7 = (s32[1,128]{1,0:T(1,128)S(1)}, s32[1,128]{1,0:T(1,128)}, u32[]{:S(2)}) copy-start(s32[1,128]{1,0:T(1,128)} %param.11) | copy-start | bytes 1540
  63.3 20.4 %all-to-all-start.3 = ((bf16[4,128,1024]{2,1,0:T(8,128)(2,1)}), bf16[4,128,1024]{2,1,0:T(8,128)(2,1)S(1)}, u32[]{:S(2)}, u32[]{:S(2)}) async-start(bf16[4,128,1024]{2,1,0:T(8,128)(2,1)} %copy.51), calls=%async_computation.3 | async-start | bytes 2097152 | tf_op jit(solution)/shard_map/all_to_all | solution.py:18
  70.5 2.4 %copy-start.5 = (bf16[128,4,4,256]{3,0,1,2:T(8,128)(2,1)S(1)}, bf16[128,4,4,256]{3,0,1,2:T(8,128)(2,1)}, u32[]{:S(2)}) copy-start(bf16[128,4,4,256]{3,0,1,2:T(8,128)(2,1)} %copy.44) | copy-start | bytes 3145732
  72.8 2.8 %copy-start.6 = (bf16[128,4,4,256]{3,0,1,2:T(8,128)(2,1)S(1)}, bf16[128,4,4,256]{3,0,1,2:T(8,128)(2,1)}, u32[]{:S(2)}) copy-start(bf16[128,4,4,256]{3,0,1,2:T(8,128)(2,1)} %copy.43) | copy-start | bytes 3145732
  75.6 2.5 %copy-start.1 = (bf16[1,128,2048]{2,1,0:T(8,128)(2,1)S(1)}, bf16[1,128,2048]{2,1,0:T(8,128)(2,1)}, u32[]{:S(2)}) copy-start(bf16[1,128,2048]{2,1,0:T(8,128)(2,1)} %param.7) | copy-start | bytes 1572868
  75.6 2.5 %copy-start.2 = (bf16[1,128,2048]{2,1,0:T(8,128)(2,1)S(1)}, bf16[1,128,2048]{2,1,0:T(8,128)(2,1)}, u32[]{:S(2)}) copy-start(bf16[1,128,2048]{2,1,0:T(8,128)(2,1)} %param.9) | copy-start | bytes 1572868
  82.4 5.1 %collective-permute-start.3 = (bf16[128,1024]{1,0:T(8,128)(2,1)S(1)}, bf16[128,1024]{1,0:T(8,128)(2,1)S(1)}, u32[]{:S(2)}, u32[]{:S(2)}) collective-permute-start(bf16[128,1024]{1,0:T(8,128)(2,1)S(1)} %pad_maximum_fusion.11), channel_id=1, source_target_pairs={{16,0},{32,16},{48,32},{64,48},{80,64},{96,80},{112,96},{128,112},... | collective-permute-start | bytes 786440 | tf_op jit(solution)/shard_map/ppermute | solution.py:27
  83.7 22.0 %collective-permute-start.4 = (bf16[512,1024]{1,0:T(8,128)(2,1)S(1)}, bf16[512,1024]{1,0:T(8,128)(2,1)}, u32[]{:S(2)}, u32[]{:S(2)}) collective-permute-start(bf16[512,1024]{1,0:T(8,128)(2,1)S(1)} %bitcast.51), channel_id=1, source_target_pairs={{0,16},{16,0},{1,17},{17,1},{2,18},{18,2},{3,19},{19,3},{4,20},{20... | collective-permute-start | bytes 3145736 | tf_op jit(solution)/shard_map/ppermute | solution.py:31
  179.5 3.2 %collective-permute-start.5 = (bf16[256,256]{1,0:T(8,128)(2,1)S(1)}, bf16[256,256]{1,0:T(8,128)(2,1)S(1)}, u32[]{:S(2)}, u32[]{:S(2)}) collective-permute-start(bf16[256,256]{1,0:T(8,128)(2,1)S(1)} %bitcast.56), channel_id=1, source_target_pairs={{0,16},{16,0},{1,17},{17,1},{2,18},{18,2},{3,19},{19,3},{4,20},{20... | collective-permute-start | bytes 393224 | tf_op jit(solution)/shard_map/ppermute | solution.py:31
